TPU v7x, 256 devices: a whole 4x4x8 slice. The times are simulated.
256 devices in a mesh: gx: 8 (over z), gy: 16 (over y, x), sa: 2 (over core).
Axes of the slice: x: 4, y: 4, z: 8, core: 2. Of those that a mesh axis runs over, the one named last changes fastest.
Arguments:
- field: float32 [33, 32, 672, 256], P(None, 'gx', 'gy', 'sa'), as said below
- start: float32 [33, 16], replicated, may hold values from -1 to 1
Outputs:
- basis: float32 [33, 16], replicated
- gram_two: float32 [672, 672], P('gy', ('gx', 'sa'))
Inputs may be any that keep to these rules, and one draw needn't show every extreme that they name: `field`: every entry is finite; species differ in scale.
All inputs are finite; a program needn't handle non-finite values.
Results may differ from a plain program's by a relative error of at most 0.0003.
Values sent between devices are 32-bit elements; how exact they have to be, the bound alone decides.
A program may use at most 128 MiB of HBM per device.

v0:
```python
import jax
import jax.numpy as jnp
from jax import lax
from jax.sharding import PartitionSpec as P

ITERS = 4
HIGH = lax.Precision.HIGHEST


def orth(block):
    inner = jnp.dot(block.T, block, precision=HIGH, preferred_element_type=jnp.float32)
    lower = jnp.linalg.cholesky(inner)
    return jax.scipy.linalg.solve_triangular(lower, block.T, lower=True).T


def leading(gram, start, rounds):
    basis = orth(orth(start))
    for step in range(rounds):
        basis = orth(orth(jnp.dot(gram, basis, precision=HIGH, preferred_element_type=jnp.float32)))
    return basis


def project(basis, data):
    return jnp.einsum("sr,sxyz->rxyz", basis, data, precision=HIGH)


def line_gram(left, right):
    return jnp.einsum("rxiz,rxjz->ij", left, right, precision=HIGH)


def on_device(field, start):
    species, cells_x, cells_y, cells_z = field.shape
    ranks = start.shape[1]
    total_x = cells_x * lax.axis_size("gx")
    total_y = cells_y * lax.axis_size("gy")
    total_z = cells_z * lax.axis_size("sa")
    flat = field.reshape(species, -1)
    partial_gram = jnp.dot(flat, flat.T, precision=HIGH, preferred_element_type=jnp.float32)
    species_gram = lax.psum(partial_gram, ("gx", "gy", "sa")) / (total_x * total_y * total_z)
    basis = leading(species_gram, start, ITERS)
    core = project(basis, field)
    part_block = line_gram(core, lax.all_gather(core, "gy", axis=2, tiled=True))
    block = lax.psum_scatter(part_block, ("gx", "sa"), scatter_dimension=1, tiled=True) / (
        ranks * total_x * total_z
    )
    return (basis, block)


def solution(mesh):
    in_specs = (P(None, "gx", "gy", "sa"), P())
    out_specs = (P(), P("gy", ("gx", "sa")))
    return jax.shard_map(
        on_device, mesh=mesh, in_specs=in_specs, out_specs=out_specs, check_vma=False
    )
```

profile of v0, /device:TPU:1, one launch (start us, length us, event | category | flops | bytes accessed | tf_op | source)
XLA Modules:
  0.0 422.5 jit_solution(17980562996375337005)
XLA Ops:
  7.2 0.6 copy-done
  8.1 1.5 cholesky.164
  9.6 0.6 compare_reduce_fusion.9
  10.2 0.6 fusion.27
  10.9 1.2 custom-call.14
  12.5 1.5 cholesky.175
  14.0 0.6 compare_reduce_fusion.8
  14.7 0.6 fusion.28
  15.3 1.2 custom-call.15
  16.8 6.2 %fusion.12 = f32[33,33]{1,0:T(8,128)S(1)} fusion(f32[33,4,42,128]{3,1,2,0:T(4,128)} %param.5), kind=kOutput, calls=%fused_computation.8 | convolution fusion | flops 281014272 | bytes 2842884 | tf_op jit(solution)/shard_map/dot_general | solution.py:38
  22.9 81.5 %psum.7 = f32[33,33]{1,0:T(8,128)S(1)} all-reduce(f32[33,33]{1,0:T(8,128)S(1)} %fusion.12), channel_id=1, replica_groups=mesh['gx'=8,'gy'=16,'sa'=2] {'gx','gy','sa'}, use_global_device_ids=true, to_apply=%region_0.0 | all-reduce | flops 1089 | bytes 8712 | tf_op jit(solution)/shard_map/psum | solution.py:39
  104.8 1.5 cholesky.186
  106.3 0.6 compare_reduce_fusion.7
  107.0 0.6 fusion.29
  107.6 1.2 custom-call.16
  109.3 1.5 cholesky.197
  110.8 0.6 compare_reduce_fusion.6
  111.4 0.6 fusion.30
  112.1 1.2 custom-call.17
  113.9 1.5 cholesky.208
  115.4 0.6 compare_reduce_fusion.5
  116.0 0.6 fusion.31
  116.7 1.2 custom-call.18
  118.4 1.5 cholesky.219
  119.9 0.6 compare_reduce_fusion.4
  120.5 0.6 fusion.32
  121.2 1.2 custom-call.19
  123.0 1.5 cholesky.230
  124.5 0.6 compare_reduce_fusion.3
  125.1 0.6 fusion.33
  125.8 1.2 custom-call.20
  127.4 1.5 cholesky.241
  128.9 0.6 compare_reduce_fusion.2
  129.6 0.6 fusion.34
  130.2 1.2 custom-call.21
  132.0 1.5 cholesky.252
  133.5 0.6 compare_reduce_fusion.1
  134.2 0.6 fusion.35
  134.9 1.2 custom-call.22
  136.5 1.5 cholesky.263
  138.0 0.6 compare_reduce_fusion
  138.7 0.6 fusion.36
  139.3 1.2 custom-call.23
  140.8 3.4 fusion.2
  144.4 138.0 %all-gather.2.cloned.1.call-done = f32[16,4,672,128]{3,0,2,1:T(8,128)} async-done(((f32[16,4,42,128]{3,0,2,1:T(8,128)}), f32[16,4,672,128]{3,0,2,1:T(8,128)}) %all-gather.2.cloned.1.call-update) | async-done | bytes 22020112 | tf_op jit(solution)/shard_map/all_gather | solution.py:42
  282.4 29.2 %fusion.7 = f32[42,672]{1,0:T(8,128)} fusion(f32[16,4,672,128]{3,0,2,1:T(8,128)} %all-gather.2.cloned.1.call-done, f32[16,4,42,128]{3,0,2,1:T(8,128)} %fusion.2), kind=kOutput, calls=%fused_computation.7 | convolution fusion | flops 2774532096 | bytes 23509248 | tf_op jit(solution)/shard_map/rxiz,rxjz->ij/dot_general | solution.py:28
  312.9 101.3 %all-reduce.3.cloned.1.call-done = f32[42,672]{1,0:T(8,128)} async-done(((f32[42,672]{1,0:T(8,128)}), f32[42,672]{1,0:T(8,128)}) %all-reduce.3.cloned.1.call-update) | async-done | bytes 112912
  414.2 1.5 dynamic-slice_multiply_fusion
  (66 shorter events, 6.0 us)
Async XLA Ops:
  7.2 0.7 copy-start
  7.2 133.6 %copy-start.1 = (f32[33,4,42,128]{3,1,2,0:T(4,128)S(1)}, f32[33,4,42,128]{3,1,2,0:T(4,128)}, u32[]{:S(2)}) copy-start(f32[33,4,42,128]{3,1,2,0:T(4,128)} %param.5) | copy-start | bytes 8515588
  7.2 275.2 %all-gather.2.cloned.1.call-start = ((), (), s32[]{:S(2)}) async-start(), calls=%async_computation | async-start | bytes 23396352 | tf_op jit(solution)/shard_map/all_gather | solution.py:42
  140.7 3.4 copy-start.2
  144.2 167.4 %copy-start.3 = (u32[256]{0:T(256)S(1)}, u32[256]{0:T(256)}, u32[]{:S(2)}) copy-start(u32[256]{0:T(256)} %constant.40) | copy-start | bytes 3076
  144.2 270.0 %all-reduce.3.cloned.1.call-start = ((), (), s32[]{:S(2)}) async-start(), calls=%async_computation.1 | async-start | bytes 294912
Sparse Core Ops, SparseCore 0:
  144.3 138.0 all-gather.1
  311.7 102.3 all-reduce.2
where the time goes:
time: 423 us; the launch traced here: 422 us
  waiting for transfers between devices  239 us (57%)
  blocking collectives  81.5 us (19%)
  matrix products  42.7 us (10%)
  other arithmetic  41.8 us (10%)
  between operations  14.9 us (4%)
    all_gather x1, waiting for transfers between devices, on_device(): part_block = line_gram(core, lax.all_gather(core, 'gy', axis=2, tiled=True))  138 us
    unnamed x3, waiting for transfers between devices  101 us
    psum x1, blocking collectives, on_device(): lax.psum(partial_gram, ('gx', 'gy', 'sa')) / (total_x * total_y * total_z)  81.5 us
    dot_general x1, matrix products, line_gram(): return jnp.einsum('rxiz,rxjz->ij', left, right, precision=HIGH)  29.2 us
    another operation x30, other arithmetic, orth(): lower = jnp.linalg.cholesky(inner)  21.5 us
    another operation x20, other arithmetic, orth(): return jax.scipy.linalg.solve_triangular(lower, block.T, lower=True).T  18.8 us
  transfers between devices with their start and end apart: 2, of which 2 were waited for; matrix products, arithmetic and copies ran while one was open for 0% of the time, Pallas kernels for 0%

commit v1 on v0

--- a/solution.py
+++ b/solution.py
@@ -39,7 +39,12 @@
     species_gram = lax.psum(partial_gram, ("gx", "gy", "sa")) / (total_x * total_y * total_z)
     basis = leading(species_gram, start, ITERS)
     core = project(basis, field)
-    part_block = line_gram(core, lax.all_gather(core, "gy", axis=2, tiled=True))
+    part_block = line_gram(
+        core,
+        jnp.concatenate(
+            lax.all_to_all(jnp.stack([core] * lax.axis_size("gy")), "gy", 0, 0), axis=2
+        ),
+    )
     block = lax.psum_scatter(part_block, ("gx", "sa"), scatter_dimension=1, tiled=True) / (
         ranks * total_x * total_z
     )

time: 423 us -> 541 us (1.28)
  blocking collectives: 81.5 us -> 327 us
  waiting for transfers between devices: 239 us -> 98 us
  local copies, waits for them, and re-layouts: 1.98 us -> 19.6 us
    all_to_all x0 -> x1, blocking collectives: none -> 245 us  [on_device(): lax.all_to_all(jnp.stack([core] * lax.axis_size('gy')), 'gy', 0, 0)]
    all_gather x1 -> x0, waiting for transfers between devices: 138 us -> none  [on_device(): part_block = line_gram(core, lax.all_gather(core, 'gy', axis=2, tiled=True))]
    another operation x0 -> x1, local copies, waits for them, and re-layouts: none -> 9.98 us  [on_device(): jnp.stack([core] * lax.axis_size('gy'))]
    all_to_all x0 -> x1, local copies, waits for them, and re-layouts: none -> 7.62 us  [on_device(): lax.all_to_all(jnp.stack([core] * lax.axis_size('gy')), 'gy', 0, 0)]
    unnamed x3 -> x2, waiting for transfers between devices: 101 us -> 98 us
  transfers between devices with their start and end apart: 2 -> 1, of which waited for: 2 -> 1; matrix products, arithmetic and copies ran while one was open for 0% -> 0% of each run, Pallas kernels for 0% -> 0%
where the time goes in v1:
time: 541 us
  blocking collectives  327 us (60%)
  waiting for transfers between devices  98 us (18%)
  other arithmetic  41.8 us (8%)
  matrix products  39.9 us (7%)
  local copies, waits for them, and re-layouts  19.6 us (4%)
  between operations  14.9 us (3%)
    all_to_all x1, blocking collectives, on_device(): lax.all_to_all(jnp.stack([core] * lax.axis_size('gy')), 'gy', 0, 0)  245 us
    unnamed x2, waiting for transfers between devices  98 us
    psum x1, blocking collectives, on_device(): lax.psum(partial_gram, ('gx', 'gy', 'sa')) / (total_x * total_y * total_z)  81.7 us
    dot_general x1, matrix products, line_gram(): return jnp.einsum('rxiz,rxjz->ij', left, right, precision=HIGH)  27.4 us
    another operation x30, other arithmetic, orth(): lower = jnp.linalg.cholesky(inner)  21.5 us
    another operation x20, other arithmetic, orth(): return jax.scipy.linalg.solve_triangular(lower, block.T, lower=True).T  18.8 us
  transfers between devices with their start and end apart: 1, of which 1 were waited for; matrix products, arithmetic and copies ran while one was open for 0% of the time, Pallas kernels for 0%

profile of v1, /device:TPU:1, one launch (start us, length us, event | category | flops | bytes accessed | tf_op | source)
XLA Modules:
  0.0 540.7 jit_solution(8105629635832154136)
XLA Ops:
  8.1 1.5 cholesky.164
  9.6 0.6 compare_reduce_fusion.9
  10.2 0.6 fusion.27
  10.9 1.2 custom-call.14
  12.5 1.5 cholesky.175
  14.0 0.6 compare_reduce_fusion.8
  14.7 0.6 fusion.28
  15.3 1.2 custom-call.15
  16.8 6.2 %fusion.12 = f32[33,33]{1,0:T(8,128)S(1)} fusion(f32[33,4,42,128]{3,1,2,0:T(4,128)} %param.5), kind=kOutput, calls=%fused_computation.8 | convolution fusion | flops 281014272 | bytes 2842884 | tf_op jit(solution)/shard_map/dot_general | solution.py:38
  22.9 81.7 %psum.7 = f32[33,33]{1,0:T(8,128)S(1)} all-reduce(f32[33,33]{1,0:T(8,128)S(1)} %fusion.12), channel_id=1, replica_groups=mesh['gx'=8,'gy'=16,'sa'=2] {'gx','gy','sa'}, use_global_device_ids=true, to_apply=%region_0.0 | all-reduce | flops 1089 | bytes 8712 | tf_op jit(solution)/shard_map/psum | solution.py:39
  105.0 1.5 cholesky.186
  106.5 0.6 compare_reduce_fusion.7
  107.2 0.6 fusion.29
  107.8 1.2 custom-call.16
  109.5 1.5 cholesky.197
  111.0 0.6 compare_reduce_fusion.6
  111.6 0.6 fusion.30
  112.3 1.2 custom-call.17
  114.1 1.5 cholesky.208
  115.6 0.6 compare_reduce_fusion.5
  116.2 0.6 fusion.31
  116.9 1.2 custom-call.18
  118.5 1.5 cholesky.219
  120.0 0.6 compare_reduce_fusion.4
  120.7 0.6 fusion.32
  121.4 1.2 custom-call.19
  123.2 1.5 cholesky.230
  124.7 0.6 compare_reduce_fusion.3
  125.3 0.6 fusion.33
  126.0 1.2 custom-call.20
  127.6 1.5 cholesky.241
  129.1 0.6 compare_reduce_fusion.2
  129.8 0.6 fusion.34
  130.4 1.2 custom-call.21
  132.2 1.5 cholesky.252
  133.7 0.6 compare_reduce_fusion.1
  134.4 0.6 fusion.35
  135.0 1.2 custom-call.22
  136.7 1.5 cholesky.263
  138.8 0.6 fusion.36
  139.5 1.2 custom-call.23
  141.0 2.3 fusion.2
  143.2 10.0 %stack.2 = f32[16,16,4,42,128]{4,1,3,2,0:T(8,128)} broadcast(f32[16,4,42,128]{3,0,2,1:T(8,128)S(1)} %fusion.2), dimensions={1,2,3,4} | broadcast | bytes 23396352 | tf_op jit(solution)/shard_map/stack | solution.py:45
  153.2 244.8 %all_to_all.5 = f32[16,16,4,42,128]{4,1,3,2,0:T(8,128)S(1)} all-to-all(f32[16,16,4,42,128]{4,1,3,2,0:T(8,128)} %stack.2), channel_id=1, replica_groups=mesh['gx'=8,'gy'=16,'sa'=2] {'gy'}, dimensions={0} | all-to-all | bytes 44040192 | tf_op jit(solution)/shard_map/all_to_all | solution.py:45
  398.0 7.6 %copy.47 = f32[16,16,4,42,128]{4,1,3,0,2:T(8,128)} copy(f32[16,16,4,42,128]{4,1,3,2,0:T(8,128)S(1)} %all_to_all.5) | data formatting | bytes 44040192 | tf_op jit(solution)/shard_map/all_to_all | solution.py:45
  405.7 27.4 %fusion.7 = f32[42,672]{1,0:T(8,128)} fusion(f32[16,4,672,128]{3,0,2,1:T(8,128)} %bitcast.154, f32[16,4,42,128]{3,0,2,1:T(8,128)S(1)} %fusion.2), kind=kOutput, calls=%fused_computation.7 | convolution fusion | flops 2774532096 | bytes 23509248 | tf_op jit(solution)/shard_map/rxiz,rxjz->ij/dot_general | solution.py:28
  434.4 98.0 %all-reduce.3.cloned.1.call-done = f32[42,672]{1,0:T(8,128)} async-done(((f32[42,672]{1,0:T(8,128)}), f32[42,672]{1,0:T(8,128)}) %all-reduce.3.cloned.1.call-update) | async-done | bytes 112912
  532.3 1.5 dynamic-slice_multiply_fusion
  (68 shorter events, 7.1 us)
Async XLA Ops:
  7.2 0.7 copy-start
  7.2 133.8 %copy-start.2 = (f32[33,4,42,128]{3,1,2,0:T(4,128)S(1)}, f32[33,4,42,128]{3,1,2,0:T(4,128)}, u32[]{:S(2)}) copy-start(f32[33,4,42,128]{3,1,2,0:T(4,128)} %param.5) | copy-start | bytes 8515588
  7.2 525.1 %all-reduce.3.cloned.1.call-start = ((), (), s32[]{:S(2)}) async-start(), calls=%async_computation.1 | async-start | bytes 294912
  140.9 12.3 %copy-start.3 = (f32[16,33]{1,0:T(8,128)}, f32[16,33]{1,0:T(8,128)S(1)}, u32[]{:S(2)}) copy-start(f32[16,33]{1,0:T(8,128)S(1)} %fusion.38) | copy-start | bytes 6340
  405.7 27.5 %copy-start.4 = (u32[256]{0:T(256)S(1)}, u32[256]{0:T(256)}, u32[]{:S(2)}) copy-start(u32[256]{0:T(256)} %constant.40) | copy-start | bytes 3076
  405.7 128.2 %copy-start.1 = (f32[33,16]{0,1:T(8,128)S(1)}, f32[33,16]{0,1:T(8,128)}, u32[]{:S(2)}) copy-start(f32[33,16]{0,1:T(8,128)} %param.6) | copy-start | bytes 6340
Sparse Core Ops, SparseCore 0:
  433.2 99.0 all-reduce.2
